TPU v7x, 32 devices: a whole 2x2x4 slice. The times are simulated.
32 devices in a mesh: band: 2 (over core), grid: 16 (over z, y, x).
Axes of the slice: x: 2, y: 2, z: 4, core: 2. Of those that a mesh axis runs over, the one named last changes fastest.
Arguments:
- coefficients: float32 [4, 2, 128, 128, 128], P('band', None, 'grid'), may hold values from -0.01171875 to 0.01171875
- potential: float32 [128, 128, 128], P('grid'), may hold values from -3 to 3
- external: float32 [128, 128, 128], P('grid'), may hold values from -6 to 6
- core_density: float32 [128, 128, 128], P('grid'), may hold values from 0.05 to 0.5
- rotations: float32 [2, 4, 2], P(None, 'band'), may hold values from -2 to 3
- mlp_in: float32 [3, 32], replicated, may hold values from -4 to 4
- mlp_out: float32 [32], replicated, may hold values from -0.4 to 0.4
Outputs:
- new_coefficients: float32 [4, 2, 128, 128, 128], P('band', None, 'grid')
- new_potential: float32 [128, 128, 128], P('grid')
All inputs are finite; a program needn't handle non-finite values.
Results may differ from a plain program's by a relative error of at most 0.0003.
Values sent between devices are 32-bit elements; how exact they have to be, the bound alone decides.
A program may use at most 64 MiB of HBM per device.

v0:
```python
import math
import jax
import jax.numpy as jnp
from jax import lax
from jax.sharding import PartitionSpec as P

NX = 128
NY = 128
NZ = 128
ITERS = 2
step_size = 0.2
epsilon = 1e-06
spacing = 0.58
kinetic_scale = 0.5 * (2.0 * math.pi / spacing) ** 2
coulomb_scale = spacing * spacing / math.pi
gradient_scale = 2.0 * math.pi / spacing
reduced_scale = 2.0 * (3.0 * math.pi * math.pi) ** (1.0 / 3.0)
exchange_scale = (3.0 / math.pi) ** (1.0 / 3.0)


def frequencies(points, offset, length):
    places = offset + lax.iota(jnp.int32, length)
    return jnp.where(2 * places < points, places, places - points)


def without_nyquist(values, points):
    return jnp.where(2 * values == -points, 0, values)


def reciprocal_tables(offset, length):
    along_x = frequencies(NX, offset, length)
    along_y = frequencies(NY, 0, NY)
    raw_z = frequencies(NZ, 0, NZ)
    along_z = raw_z * (NX // NZ)
    squared = (
        along_x[:, None, None] * along_x[:, None, None]
        + along_y[None, :, None] * along_y[None, :, None]
        + along_z[None, None, :] * along_z[None, None, :]
    )
    cutoff = (16 * squared <= NX * NX).astype(jnp.float32)
    kinetic = kinetic_scale * squared.astype(jnp.float32) / (NX * NX)
    coulomb = jnp.where(
        squared > 0, coulomb_scale * (NX * NX) / jnp.maximum(squared, 1).astype(jnp.float32), 0.0
    )
    slope_x = gradient_scale * without_nyquist(along_x, NX).astype(jnp.float32) / NX
    slope_y = gradient_scale * without_nyquist(along_y, NY).astype(jnp.float32) / NX
    slope_z = gradient_scale * (without_nyquist(raw_z, NZ) * (NX // NZ)).astype(jnp.float32) / NX
    return (
        cutoff,
        kinetic,
        coulomb,
        slope_x[:, None, None],
        slope_y[None, :, None],
        slope_z[None, None, :],
    )


def dft_tables(points, direction):
    places = lax.iota(jnp.int32, points)
    phases = places[:, None] * places[None, :] % points
    angles = phases.astype(jnp.float32) * (2.0 * math.pi / points)
    return (jnp.cos(angles), direction * jnp.sin(angles))


def transform(perceptron_levels, tables, pattern):
    highest = lax.Precision.HIGHEST
    cosine_table, sine_table = tables
    real_part = perceptron_levels[:, 0]
    imag_part = perceptron_levels[:, 1]
    new_real = jnp.einsum(pattern, real_part, cosine_table, precision=highest) - jnp.einsum(
        pattern, imag_part, sine_table, precision=highest
    )
    new_imag = jnp.einsum(pattern, real_part, sine_table, precision=highest) + jnp.einsum(
        pattern, imag_part, cosine_table, precision=highest
    )
    return jnp.stack([new_real, new_imag], 1)


def toward_position_grid(spectral_amplitude, fourier_synthesis, orbital_holder):
    perceptron_levels = transform(spectral_amplitude, fourier_synthesis[2], "bxyz,zw->bxyw")
    perceptron_levels = transform(perceptron_levels, fourier_synthesis[1], "bxyz,yv->bxvz")
    perceptron_levels = orbital_holder(perceptron_levels)
    return transform(perceptron_levels, fourier_synthesis[0], "bxyz,xu->byuz")


def toward_spectral_amplitudes(position_grid_values, fourier_analysis, orbital_holder):
    perceptron_levels = transform(position_grid_values, fourier_analysis[0], "byxz,xu->buyz")
    perceptron_levels = orbital_holder(perceptron_levels)
    perceptron_levels = transform(perceptron_levels, fourier_analysis[1], "bxyz,yv->bxvz")
    perceptron_levels = transform(perceptron_levels, fourier_analysis[2], "bxyz,zw->bxyw")
    return perceptron_levels / (NX * NY * NZ)


def body(coefficients, potential, external, core_density, rotations, mlp_in, mlp_out):
    highest = lax.Precision.HIGHEST
    planes = coefficients.shape[2]
    offset = lax.axis_index("grid") * planes
    cutoff, kinetic, coulomb, slope_x, slope_y, slope_z = reciprocal_tables(offset, planes)
    fourier_synthesis = (dft_tables(NX, 1.0), dft_tables(NY, 1.0), dft_tables(NZ, 1.0))
    fourier_analysis = (dft_tables(NX, -1.0), dft_tables(NY, -1.0), dft_tables(NZ, -1.0))

    def outward(perceptron_levels):
        return lax.all_to_all(perceptron_levels, "grid", split_axis=3, concat_axis=2, tiled=True)

    def inward(perceptron_levels):
        return lax.all_to_all(perceptron_levels, "grid", split_axis=2, concat_axis=3, tiled=True)

    current = cutoff * coefficients
    for iteration in range(ITERS):
        applied = cutoff * (
            kinetic * current
            + toward_spectral_amplitudes(
                toward_position_grid(current, fourier_synthesis, outward) * potential,
                fourier_analysis,
                inward,
            )
        )
        rotation = rotations[iteration]
        intersection, energy = lax.psum(
            (
                jnp.sum(current * current, axis=(1, 2, 3, 4)),
                jnp.sum(current * applied, axis=(1, 2, 3, 4)),
            ),
            "grid",
        )
        factor = 1.0 + step_size * (energy / (intersection + epsilon))
        updated = factor[:, None, None, None, None] * current - step_size * applied
        updated = jnp.einsum("ij,jcxyz->icxyz", rotation, updated, precision=highest)
        length = lax.psum(jnp.sum(updated * updated, axis=(1, 2, 3, 4)), "grid")
        current = updated / jnp.sqrt(length + epsilon)[:, None, None, None, None]
    real_space = toward_position_grid(current, fourier_synthesis, outward)
    bands_all = coefficients.shape[0] * lax.axis_size("band")
    partial_value = 2.0 / bands_all * jnp.sum(real_space * real_space, axis=(0, 1))
    density = lax.psum(partial_value, "band") + core_density
    spectrum = toward_spectral_amplitudes(
        jnp.stack([density, jnp.zeros_like(density)])[None], fourier_analysis, inward
    )[0]
    spec_real = spectrum[0]
    spec_imag = spectrum[1]
    first_real = coulomb * spec_real - slope_x * spec_real
    first_imag = coulomb * spec_imag - slope_x * spec_imag
    second_real = -slope_y * spec_imag - slope_z * spec_real
    second_imag = slope_y * spec_real - slope_z * spec_imag
    fields = toward_position_grid(
        jnp.stack([jnp.stack([first_real, first_imag]), jnp.stack([second_real, second_imag])]),
        fourier_synthesis,
        outward,
    )
    hartree = fields[0, 0]
    change_x = fields[0, 1]
    change_y = fields[1, 0]
    change_z = fields[1, 1]
    cube_root = jnp.cbrt(density)
    gradient = jnp.sqrt(change_x * change_x + change_y * change_y + change_z * change_z)
    reduced = gradient / (reduced_scale * density * cube_root)
    bounded = reduced / (1.0 + reduced)
    hidden = jnp.tanh(
        mlp_in[0][:, None, None, None] * cube_root
        + mlp_in[1][:, None, None, None] * bounded
        + mlp_in[2][:, None, None, None]
    )
    enhance = 1.0 + jnp.einsum("k,kyxz->yxz", mlp_out, hidden, precision=highest)
    new_potential = external + hartree - exchange_scale * cube_root * enhance
    return (current, new_potential)


def solution(mesh):
    in_specs = (
        P("band", None, "grid", None, None),
        P("grid", None, None),
        P("grid", None, None),
        P("grid", None, None),
        P(None, "band", None),
        P(),
        P(),
    )
    out_specs = (P("band", None, "grid", None, None), P("grid", None, None))
    return jax.shard_map(body, mesh=mesh, in_specs=in_specs, out_specs=out_specs, check_vma=False)
```

profile of v0, /device:TPU:12, one launch (start us, length us, event | category | flops | bytes accessed | tf_op | source)
XLA Modules:
  0.0 682.6 jit_solution(3617643584464941430)
XLA Ops:
  7.5 1.9 copy_multiply_fusion
  11.9 1.3 fusion.152
  16.9 1.3 fusion.38
  18.2 1.3 fusion.39
  21.0 54.6 %all_to_all.126 = f32[2,2,8,128,128]{4,2,0,1,3:T(8,128)S(1)} all-to-all(f32[2,2,8,128,128]{4,2,0,1,3:T(8,128)S(1)} %copy.58), channel_id=1, replica_groups=mesh['band'=2,'grid'=16] {'grid'}, dimensions={3} | all-to-all | bytes 4194304 | tf_op jit(solution)/shard_map/all_to_all | solution.py:103
  75.8 1.3 fusion.51
  78.4 1.3 fusion.36
  79.8 1.4 fusion.37
  81.4 1.3 fusion.53
  84.0 1.3 fusion.34
  85.3 1.3 fusion.35
  86.8 2.5 copy.60
  89.4 16.6 %all-to-all-start.1 = ((f32[2,2,128,8,128]{4,3,0,1,2:T(8,128)}), f32[2,2,128,8,128]{4,3,0,1,2:T(8,128)S(1)}, u32[]{:S(2)}, u32[]{:S(2)}) async-start(f32[2,2,128,8,128]{4,3,0,1,2:T(8,128)} %copy.60), calls=%async_computation.1 | async-start | bytes 4194304 | tf_op jit(solution)/shard_map/all_to_all | solution.py:106
  106.2 46.5 %all-to-all-done.1 = f32[2,2,128,8,128]{4,3,0,1,2:T(8,128)S(1)} async-done(((f32[2,2,128,8,128]{4,3,0,1,2:T(8,128)}), f32[2,2,128,8,128]{4,3,0,1,2:T(8,128)S(1)}, u32[]{:S(2)}, u32[]{:S(2)}) %all-to-all-start.1) | async-done | bytes 2097184 | tf_op jit(solution)/shard_map/all_to_all | solution.py:106
  153.0 1.3 fusion.55
  155.6 1.3 fusion.33
  164.8 29.5 %all-reduce.2 = (f32[2]{0:T(128)S(1)}, f32[2]{0:T(128)S(1)}) all-reduce(f32[2]{0:T(128)S(1)} %get-tuple-element.9, f32[2]{0:T(128)S(1)} %get-tuple-element.8), channel_id=1, replica_groups=mesh['band'=2,'grid'=16] {'grid'}, use_global_device_ids=true, to_apply=%region_1.2 | all-reduce | flops 4 | bytes 32 | tf_op jit(solution)/shard_map/psum | solution.py:119
  194.3 2.3 multiply_subtract_fusion.1
  196.7 9.5 %multiply_reduce_fusion.3 = (f32[2]{0:T(128)S(1)}, f32[2,8,128,128,2]{3,4,2,1,0:T(2,128)S(1)}) fusion(f32[2,2,2]{2,1,0:T(2,128)S(1)} %copy-done.11, f32[2,2,8,128,128]{4,3,2,0,1:T(8,128)S(1)} %multiply_subtract_fusion.1), kind=kOutput, calls=%fused_computation.35 | convolution fusion | flops 13631486 | bytes 4195336 | tf_op jit(solution)/shard_map/ij,jcxyz->icxyz/dot_general | solution.py:128
  206.1 37.0 %psum.51 = f32[2]{0:T(128)S(1)} all-reduce(f32[2]{0:T(128)S(1)} %get-tuple-element.27), channel_id=1, replica_groups=mesh['band'=2,'grid'=16] {'grid'}, use_global_device_ids=true, to_apply=%region_5.6 | all-reduce | flops 2 | bytes 16 | tf_op jit(solution)/shard_map/psum | solution.py:129
  251.0 1.3 fusion.28
  252.3 1.3 fusion.29
  255.1 44.4 %all_to_all.127 = f32[2,2,8,128,128]{4,2,0,1,3:T(8,128)S(1)} all-to-all(f32[2,2,8,128,128]{4,2,0,1,3:T(8,128)S(1)} %copy.72), channel_id=1, replica_groups=mesh['band'=2,'grid'=16] {'grid'}, dimensions={3} | all-to-all | bytes 4194304 | tf_op jit(solution)/shard_map/all_to_all | solution.py:103
  299.8 1.3 fusion.59
  302.4 1.3 fusion.26
  303.7 1.4 fusion.27
  305.4 1.3 fusion.61
  307.9 1.3 fusion.24
  309.3 1.3 fusion.25
  312.0 45.8 %all_to_all.128 = f32[2,2,128,8,128]{4,3,0,1,2:T(8,128)S(1)} all-to-all(f32[2,2,128,8,128]{4,3,0,1,2:T(8,128)S(1)} %copy.74), channel_id=1, replica_groups=mesh['band'=2,'grid'=16] {'grid'}, dimensions={2} | all-to-all | bytes 4194304 | tf_op jit(solution)/shard_map/all_to_all | solution.py:106
  358.0 1.3 fusion.63
  360.6 1.3 fusion.23
  364.4 1.3 fusion.22
  369.3 29.9 %all-reduce.1 = (f32[2]{0:T(128)S(1)}, f32[2]{0:T(128)S(1)}) all-reduce(f32[2]{0:T(128)S(1)} %get-tuple-element.7, f32[2]{0:T(128)S(1)} %get-tuple-element.6), channel_id=1, replica_groups=mesh['band'=2,'grid'=16] {'grid'}, use_global_device_ids=true, to_apply=%region_7.8 | all-reduce | flops 4 | bytes 32 | tf_op jit(solution)/shard_map/psum | solution.py:119
  399.1 2.3 multiply_subtract_fusion
  401.4 9.9 %multiply_reduce_fusion = (f32[2]{0:T(128)S(1)}, f32[2,8,128,128,2]{3,4,2,1,0:T(2,128)}) fusion(f32[2,2,2]{2,1,0:T(2,128)S(1)} %copy-done.11, f32[2,2,8,128,128]{4,3,2,0,1:T(8,128)S(1)} %multiply_subtract_fusion), kind=kOutput, calls=%fused_computation.31 | convolution fusion | flops 13631486 | bytes 4195336 | tf_op jit(solution)/shard_map/ij,jcxyz->icxyz/dot_general | solution.py:128
  411.3 36.7 %psum.54 = f32[2]{0:T(128)S(1)} all-reduce(f32[2]{0:T(128)S(1)} %get-tuple-element.29), channel_id=1, replica_groups=mesh['band'=2,'grid'=16] {'grid'}, use_global_device_ids=true, to_apply=%region_11.12 | all-reduce | flops 2 | bytes 16 | tf_op jit(solution)/shard_map/psum | solution.py:129
  448.0 2.6 divide_bitcast_fusion
  458.3 1.3 fusion.19
  459.6 1.3 fusion.18
  461.1 1.4 copy.89
  462.6 44.1 %all_to_all.129 = f32[2,2,8,128,128]{4,2,0,1,3:T(8,128)S(1)} all-to-all(f32[2,2,8,128,128]{4,2,0,1,3:T(8,128)S(1)} %copy.89), channel_id=1, replica_groups=mesh['band'=2,'grid'=16] {'grid'}, dimensions={3} | all-to-all | bytes 4194304 | tf_op jit(solution)/shard_map/all_to_all | solution.py:103
  506.9 1.3 fusion.65
  509.5 1.3 fusion.16
  510.8 1.3 fusion.17
  513.2 18.1 %all-reduce.5.cloned.1.call-done = f32[8,128,128]{2,1,0:T(8,128)} async-done(((f32[8,128,128]{2,1,0:T(8,128)}), f32[8,128,128]{2,1,0:T(8,128)}) %all-reduce.5.cloned.1.call-update) | async-done | bytes 524304 | tf_op jit(solution)/shard_map/psum | solution.py:134
  531.3 2.3 fusion.639
  537.2 1.6 copy.91
  538.7 7.3 %all-to-all-start.5 = ((f32[1,2,128,8,128]{4,3,1,0,2:T(8,128)}), f32[1,2,128,8,128]{4,3,1,0,2:T(8,128)}, u32[]{:S(2)}, u32[]{:S(2)}) async-start(f32[1,2,128,8,128]{4,3,1,0,2:T(8,128)} %copy.91), calls=%async_computation.5 | async-start | bytes 2097152 | tf_op jit(solution)/shard_map/all_to_all | solution.py:106
  546.1 25.3 %all-to-all-done.5 = f32[1,2,128,8,128]{4,3,1,0,2:T(8,128)} async-done(((f32[1,2,128,8,128]{4,3,1,0,2:T(8,128)}), f32[1,2,128,8,128]{4,3,1,0,2:T(8,128)}, u32[]{:S(2)}, u32[]{:S(2)}) %all-to-all-start.5) | async-done | bytes 1048608 | tf_op jit(solution)/shard_map/all_to_all | solution.py:106
  571.4 1.3 copy.211
  584.0 1.5 fusion.137
  588.0 1.3 fusion.15
  589.3 1.3 fusion.14
  590.8 2.5 copy.101
  593.3 5.9 all-to-all-start.6
  599.3 1.6 copy.103
  600.9 45.7 %all-to-all-done.6 = f32[2,2,8,128,128]{4,2,0,1,3:T(8,128)} async-done(((f32[2,2,8,128,128]{4,2,0,1,3:T(8,128)}), f32[2,2,8,128,128]{4,2,0,1,3:T(8,128)}, u32[]{:S(2)}, u32[]{:S(2)}) %all-to-all-start.6) | async-done | bytes 2097184 | tf_op jit(solution)/shard_map/all_to_all | solution.py:103
  646.6 1.8 copy.205
  648.4 1.3 fusion.67
  652.3 1.4 fusion.13
  654.4 4.3 add_tanh_fusion
  658.8 15.2 %fusion = f32[1,8,128,128]{3,0,2,1:T(1,128)S(1)} fusion(f32[32,8,128,128]{3,2,1,0:T(8,128)S(1)} %add_tanh_fusion, f32[32]{0:T(128)S(1)} %copy-done), kind=kOutput, calls=%fused_computation | convolution fusion | flops 50331648 | bytes 17301632 | tf_op jit(solution)/shard_map/k,kyxz->yxz/dot_general | solution.py:162
  674.0 1.3 fusion.85
  (119 shorter events, 73.3 us)
Async XLA Ops:
  7.2 651.6 %copy-start = (f32[32]{0:T(128)S(1)}, f32[32]{0:T(128)}, u32[]{:S(2)}) copy-start(f32[32]{0:T(128)} %param.13) | copy-start | bytes 388
  79.8 1.4 copy-start.6
  89.4 63.3 %all-to-all-start.1 = ((f32[2,2,128,8,128]{4,3,0,1,2:T(8,128)}), f32[2,2,128,8,128]{4,3,0,1,2:T(8,128)S(1)}, u32[]{:S(2)}, u32[]{:S(2)}) async-start(f32[2,2,128,8,128]{4,3,0,1,2:T(8,128)} %copy.60), calls=%async_computation.1 | async-start | bytes 4194304 | tf_op jit(solution)/shard_map/all_to_all | solution.py:106
  106.0 425.3 %all-reduce.5.cloned.1.call-start = ((), (), s32[]{:S(2)}) async-start(), calls=%async_computation.7 | async-start | bytes 1048576 | tf_op jit(solution)/shard_map/psum | solution.py:134
  161.9 2.9 copy-start.4
  161.9 2.0 copy-start.1
  163.9 1.0 copy-start.5
  194.3 2.3 copy-start.11
  303.7 1.4 copy-start.7
  366.9 2.3 copy-start.2
  368.2 1.1 copy-start.3
  512.1 19.1 %copy-start.9 = (f32[8,128,128]{2,1,0:T(8,128)S(1)}, f32[8,128,128]{2,1,0:T(8,128)}, u32[]{:S(2)}) copy-start(f32[8,128,128]{2,1,0:T(8,128)} %param.10) | copy-start | bytes 1572868
  538.7 32.7 %all-to-all-start.5 = ((f32[1,2,128,8,128]{4,3,1,0,2:T(8,128)}), f32[1,2,128,8,128]{4,3,1,0,2:T(8,128)}, u32[]{:S(2)}, u32[]{:S(2)}) async-start(f32[1,2,128,8,128]{4,3,1,0,2:T(8,128)} %copy.91), calls=%async_computation.5 | async-start | bytes 2097152 | tf_op jit(solution)/shard_map/all_to_all | solution.py:106
  593.3 6.0 copy-start.10
  593.3 53.2 %all-to-all-start.6 = ((f32[2,2,8,128,128]{4,2,0,1,3:T(8,128)}), f32[2,2,8,128,128]{4,2,0,1,3:T(8,128)}, u32[]{:S(2)}, u32[]{:S(2)}) async-start(f32[2,2,8,128,128]{4,2,0,1,3:T(8,128)} %copy.101), calls=%async_computation.6 | async-start | bytes 4194304 | tf_op jit(solution)/shard_map/all_to_all | solution.py:103
  658.8 15.3 %copy-start.8 = (f32[8,128,128]{2,1,0:T(8,128)S(1)}, f32[8,128,128]{2,1,0:T(8,128)}, u32[]{:S(2)}) copy-start(f32[8,128,128]{2,1,0:T(8,128)} %param.9) | copy-start | bytes 1572868
Sparse Core Ops, SparseCore 0:
  513.3 17.9 all-reduce.4
where the time goes:
time: 692 us; the launch traced here: 683 us
  blocking collectives  322 us (47%)
  matrix products  137 us (20%)
  waiting for transfers between devices  136 us (20%)
  starting transfers between devices  29.9 us (4%)
  other arithmetic  24 us (3%)
  local copies, waits for them, and re-layouts  18.7 us (3%)
  between operations  15.6 us (2%)
    all_to_all x3, blocking collectives, outward(): lax.all_to_all(perceptron_levels, 'grid', split_axis=3, concat_axis=2, ti...  143 us
    psum x2, blocking collectives, body(): length = lax.psum(jnp.sum(updated * updated, axis=(1, 2, 3, 4)), 'grid')  73.7 us
    all_to_all x2, waiting for transfers between devices, inward(): lax.all_to_all(perceptron_levels, 'grid', split_axis=2, concat_axis=3, ti...  71.8 us
    psum x2, blocking collectives, body(): lax.psum((jnp.sum(current * current, axis=(1, 2, 3, 4)), jnp.sum(current...  59.3 us
    all_to_all x1, blocking collectives, inward(): lax.all_to_all(perceptron_levels, 'grid', split_axis=2, concat_axis=3, ti...  45.8 us
    all_to_all x1, waiting for transfers between devices, outward(): lax.all_to_all(perceptron_levels, 'grid', split_axis=3, concat_axis=2, ti...  45.7 us
    dot_general x21, matrix products, transform(): jnp.einsum(pattern, imag_part, sine_table, precision=highest)  25.9 us
    dot_general x21, matrix products, transform(): jnp.einsum(pattern, imag_part, cosine_table, precision=highest)  25.7 us
  transfers between devices with their start and end apart: 4, of which 4 were waited for; matrix products, arithmetic and copies ran while one was open for 0% of the time, Pallas kernels for 0%

commit v1 on v0

--- a/solution.py
+++ b/solution.py
@@ -126,7 +126,10 @@
         factor = 1.0 + step_size * (energy / (intersection + epsilon))
         updated = factor[:, None, None, None, None] * current - step_size * applied
         updated = jnp.einsum("ij,jcxyz->icxyz", rotation, updated, precision=highest)
-        length = lax.psum(jnp.sum(updated * updated, axis=(1, 2, 3, 4)), "grid")
+        find_the_positions = lambda matrix: jnp.sum(
+            lax.all_gather(matrix, axis_name="grid"), axis=0
+        )
+        length = find_the_positions(jnp.sum(updated * updated, axis=(1, 2, 3, 4)))
         current = updated / jnp.sqrt(length + epsilon)[:, None, None, None, None]
     real_space = toward_position_grid(current, fourier_synthesis, outward)
     bands_all = coefficients.shape[0] * lax.axis_size("band")

time: 692 us -> 693 us (level)
    psum x2 -> x0, blocking collectives: 73.7 us -> none  [body(): length = lax.psum(jnp.sum(updated * updated, axis=(1, 2, 3, 4)), 'grid')]
    unnamed x0 -> x2, blocking collectives: none -> 73.6 us
where the time goes in v1:
time: 693 us; the launch traced here: 684 us
  blocking collectives  322 us (46%)
  matrix products  137 us (20%)
  waiting for transfers between devices  134 us (19%)
  starting transfers between devices  30.2 us (4%)
  other arithmetic  24.1 us (3%)
  local copies, waits for them, and re-layouts  20 us (3%)
  between operations  16.3 us (2%)
    all_to_all x3, blocking collectives, outward(): lax.all_to_all(perceptron_levels, 'grid', split_axis=3, concat_axis=2, ti...  143 us
    unnamed x2, blocking collectives  73.6 us
    all_to_all x2, waiting for transfers between devices, inward(): lax.all_to_all(perceptron_levels, 'grid', split_axis=2, concat_axis=3, ti...  70.6 us
    psum x2, blocking collectives, body(): lax.psum((jnp.sum(current * current, axis=(1, 2, 3, 4)), jnp.sum(current...  59.4 us
    all_to_all x1, blocking collectives, inward(): lax.all_to_all(perceptron_levels, 'grid', split_axis=2, concat_axis=3, ti...  45.8 us
    all_to_all x1, waiting for transfers between devices, outward(): lax.all_to_all(perceptron_levels, 'grid', split_axis=3, concat_axis=2, ti...  45.7 us
    dot_general x21, matrix products, transform(): jnp.einsum(pattern, imag_part, sine_table, precision=highest)  25.9 us
    dot_general x21, matrix products, transform(): jnp.einsum(pattern, imag_part, cosine_table, precision=highest)  25.7 us
  transfers between devices with their start and end apart: 4, of which 4 were waited for; matrix products, arithmetic and copies ran while one was open for 0% of the time, Pallas kernels for 0%

profile of v1, /device:TPU:12, one launch (start us, length us, event | category | flops | bytes accessed | tf_op | source)
XLA Modules:
  0.0 683.6 jit_solution(1049503798585917079)
XLA Ops:
  7.5 1.9 copy_multiply_fusion
  11.9 1.3 fusion.152
  16.9 1.3 fusion.38
  18.2 1.3 fusion.39
  21.0 54.6 %all_to_all.126 = f32[2,2,8,128,128]{4,2,0,1,3:T(8,128)S(1)} all-to-all(f32[2,2,8,128,128]{4,2,0,1,3:T(8,128)S(1)} %copy.102), channel_id=1, replica_groups=mesh['band'=2,'grid'=16] {'grid'}, dimensions={3} | all-to-all | bytes 4194304 | tf_op jit(solution)/shard_map/all_to_all | solution.py:103
  75.8 1.3 fusion.51
  78.4 1.3 fusion.36
  79.8 1.4 fusion.37
  81.4 1.3 fusion.53
  84.0 1.3 fusion.34
  85.3 1.3 fusion.35
  86.8 2.5 copy.104
  89.4 16.9 %all-to-all-start.1 = ((f32[2,2,128,8,128]{4,3,0,1,2:T(8,128)}), f32[2,2,128,8,128]{4,3,0,1,2:T(8,128)S(1)}, u32[]{:S(2)}, u32[]{:S(2)}) async-start(f32[2,2,128,8,128]{4,3,0,1,2:T(8,128)} %copy.104), calls=%async_computation.1 | async-start | bytes 4194304 | tf_op jit(solution)/shard_map/all_to_all | solution.py:106
  107.8 45.3 %all-to-all-done.1 = f32[2,2,128,8,128]{4,3,0,1,2:T(8,128)S(1)} async-done(((f32[2,2,128,8,128]{4,3,0,1,2:T(8,128)}), f32[2,2,128,8,128]{4,3,0,1,2:T(8,128)S(1)}, u32[]{:S(2)}, u32[]{:S(2)}) %all-to-all-start.1) | async-done | bytes 2097184 | tf_op jit(solution)/shard_map/all_to_all | solution.py:106
  153.3 1.3 fusion.55
  155.9 1.3 fusion.33
  165.1 29.5 %all-reduce.4 = (f32[2]{0:T(128)S(1)}, f32[2]{0:T(128)S(1)}) all-reduce(f32[2]{0:T(128)S(1)} %get-tuple-element.11, f32[2]{0:T(128)S(1)} %get-tuple-element.10), channel_id=1, replica_groups=mesh['band'=2,'grid'=16] {'grid'}, use_global_device_ids=true, to_apply=%region_1.2 | all-reduce | flops 4 | bytes 32 | tf_op jit(solution)/shard_map/psum | solution.py:119
  194.7 2.3 multiply_subtract_fusion.1
  197.0 9.5 %multiply_reduce_fusion.3 = (f32[2]{0:T(128)S(1)}, f32[2,8,128,128,2]{3,4,2,1,0:T(2,128)S(1)}) fusion(f32[2,2,2]{2,1,0:T(2,128)S(1)} %copy-done.11, f32[2,2,8,128,128]{4,3,2,0,1:T(8,128)S(1)} %multiply_subtract_fusion.1), kind=kOutput, calls=%fused_computation.35 | convolution fusion | flops 13631486 | bytes 4195336 | tf_op jit(solution)/shard_map/ij,jcxyz->icxyz/dot_general | solution.py:128
  206.7 37.0 %all-reduce.1 = f32[32]{0:T(128)S(1)} all-reduce(f32[32]{0:T(128)S(1)} %dynamic-update-slice), channel_id=2, replica_groups=mesh['band'=2,'grid'=16] {'grid'}, use_global_device_ids=true, to_apply=%add.1 | all-reduce | flops 32 | bytes 256
  251.7 1.3 fusion.28
  253.0 1.3 fusion.29
  255.7 44.4 %all_to_all.127 = f32[2,2,8,128,128]{4,2,0,1,3:T(8,128)S(1)} all-to-all(f32[2,2,8,128,128]{4,2,0,1,3:T(8,128)S(1)} %copy.116), channel_id=1, replica_groups=mesh['band'=2,'grid'=16] {'grid'}, dimensions={3} | all-to-all | bytes 4194304 | tf_op jit(solution)/shard_map/all_to_all | solution.py:103
  300.4 1.3 fusion.59
  303.0 1.3 fusion.26
  304.4 1.4 fusion.27
  306.0 1.3 fusion.61
  308.6 1.3 fusion.24
  309.9 1.3 fusion.25
  312.7 45.8 %all_to_all.129 = f32[2,2,128,8,128]{4,3,0,1,2:T(8,128)S(1)} all-to-all(f32[2,2,128,8,128]{4,3,0,1,2:T(8,128)S(1)} %copy.118), channel_id=1, replica_groups=mesh['band'=2,'grid'=16] {'grid'}, dimensions={2} | all-to-all | bytes 4194304 | tf_op jit(solution)/shard_map/all_to_all | solution.py:106
  358.7 1.3 fusion.63
  361.3 1.3 fusion.23
  365.0 1.3 fusion.22
  369.9 29.9 %all-reduce.3 = (f32[2]{0:T(128)S(1)}, f32[2]{0:T(128)S(1)}) all-reduce(f32[2]{0:T(128)S(1)} %get-tuple-element.9, f32[2]{0:T(128)S(1)} %get-tuple-element.8), channel_id=1, replica_groups=mesh['band'=2,'grid'=16] {'grid'}, use_global_device_ids=true, to_apply=%region_7.8 | all-reduce | flops 4 | bytes 32 | tf_op jit(solution)/shard_map/psum | solution.py:119
  399.8 2.3 multiply_subtract_fusion
  402.0 9.9 %multiply_reduce_fusion = (f32[2]{0:T(128)S(1)}, f32[2,8,128,128,2]{3,4,2,1,0:T(2,128)}) fusion(f32[2,2,2]{2,1,0:T(2,128)S(1)} %copy-done.11, f32[2,2,8,128,128]{4,3,2,0,1:T(8,128)S(1)} %multiply_subtract_fusion), kind=kOutput, calls=%fused_computation.31 | convolution fusion | flops 13631486 | bytes 4195336 | tf_op jit(solution)/shard_map/ij,jcxyz->icxyz/dot_general | solution.py:128
  412.2 36.7 %all-reduce.2 = f32[32]{0:T(128)S(1)} all-reduce(f32[32]{0:T(128)S(1)} %dynamic-update-slice.1), channel_id=3, replica_groups=mesh['band'=2,'grid'=16] {'grid'}, use_global_device_ids=true, to_apply=%add.2 | all-reduce | flops 32 | bytes 256
  449.0 2.6 divide_bitcast_fusion
  459.3 1.3 fusion.19
  460.6 1.3 fusion.18
  462.1 1.4 copy.133
  463.5 44.1 %all_to_all.128 = f32[2,2,8,128,128]{4,2,0,1,3:T(8,128)S(1)} all-to-all(f32[2,2,8,128,128]{4,2,0,1,3:T(8,128)S(1)} %copy.133), channel_id=1, replica_groups=mesh['band'=2,'grid'=16] {'grid'}, dimensions={3} | all-to-all | bytes 4194304 | tf_op jit(solution)/shard_map/all_to_all | solution.py:103
  507.9 1.3 fusion.65
  510.5 1.3 fusion.16
  511.8 1.3 fusion.17
  514.2 18.1 %all-reduce.7.cloned.1.call-done = f32[8,128,128]{2,1,0:T(8,128)} async-done(((f32[8,128,128]{2,1,0:T(8,128)}), f32[8,128,128]{2,1,0:T(8,128)}) %all-reduce.7.cloned.1.call-update) | async-done | bytes 524304 | tf_op jit(solution)/shard_map/psum | solution.py:137
  532.3 2.3 fusion.639
  538.2 1.6 copy.135
  539.7 7.3 %all-to-all-start.5 = ((f32[1,2,128,8,128]{4,3,1,0,2:T(8,128)}), f32[1,2,128,8,128]{4,3,1,0,2:T(8,128)}, u32[]{:S(2)}, u32[]{:S(2)}) async-start(f32[1,2,128,8,128]{4,3,1,0,2:T(8,128)} %copy.135), calls=%async_computation.5 | async-start | bytes 2097152 | tf_op jit(solution)/shard_map/all_to_all | solution.py:106
  547.1 25.3 %all-to-all-done.5 = f32[1,2,128,8,128]{4,3,1,0,2:T(8,128)} async-done(((f32[1,2,128,8,128]{4,3,1,0,2:T(8,128)}), f32[1,2,128,8,128]{4,3,1,0,2:T(8,128)}, u32[]{:S(2)}, u32[]{:S(2)}) %all-to-all-start.5) | async-done | bytes 1048608 | tf_op jit(solution)/shard_map/all_to_all | solution.py:106
  572.5 1.3 copy.255
  585.0 1.5 fusion.137
  589.0 1.3 fusion.15
  590.3 1.3 fusion.14
  591.8 2.5 copy.145
  594.3 5.9 all-to-all-start.6
  600.3 1.6 copy.147
  601.9 45.7 %all-to-all-done.6 = f32[2,2,8,128,128]{4,2,0,1,3:T(8,128)} async-done(((f32[2,2,8,128,128]{4,2,0,1,3:T(8,128)}), f32[2,2,8,128,128]{4,2,0,1,3:T(8,128)}, u32[]{:S(2)}, u32[]{:S(2)}) %all-to-all-start.6) | async-done | bytes 2097184 | tf_op jit(solution)/shard_map/all_to_all | solution.py:103
  647.6 1.8 copy.249
  649.4 1.3 fusion.67
  653.3 1.4 fusion.13
  655.4 4.3 add_tanh_fusion
  659.8 15.2 %fusion = f32[1,8,128,128]{3,0,2,1:T(1,128)S(1)} fusion(f32[32,8,128,128]{3,2,1,0:T(8,128)S(1)} %add_tanh_fusion, f32[32]{0:T(128)S(1)} %copy-done), kind=kOutput, calls=%fused_computation | convolution fusion | flops 50331648 | bytes 17301632 | tf_op jit(solution)/shard_map/k,kyxz->yxz/dot_general | solution.py:165
  675.0 1.3 fusion.85
  (130 shorter events, 74.6 us)
Async XLA Ops:
  7.2 652.6 %copy-start = (f32[32]{0:T(128)S(1)}, f32[32]{0:T(128)}, u32[]{:S(2)}) copy-start(f32[32]{0:T(128)} %param.13) | copy-start | bytes 388
  79.8 1.4 copy-start.6
  89.4 16.9 %copy-start.12 = (u32[32]{0:T(128)S(1)}, u32[32]{0:T(128)}, u32[]{:S(2)}) copy-start(u32[32]{0:T(128)} %constant.105) | copy-start | bytes 388
  89.4 63.6 %all-to-all-start.1 = ((f32[2,2,128,8,128]{4,3,0,1,2:T(8,128)}), f32[2,2,128,8,128]{4,3,0,1,2:T(8,128)S(1)}, u32[]{:S(2)}, u32[]{:S(2)}) async-start(f32[2,2,128,8,128]{4,3,0,1,2:T(8,128)} %copy.104), calls=%async_computation.1 | async-start | bytes 4194304 | tf_op jit(solution)/shard_map/all_to_all | solution.py:106
  106.3 426.0 %all-reduce.7.cloned.1.call-start = ((), (), s32[]{:S(2)}) async-start(), calls=%async_computation.7 | async-start | bytes 1048576 | tf_op jit(solution)/shard_map/psum | solution.py:137
  162.2 2.9 copy-start.4
  162.2 2.0 copy-start.1
  164.2 1.0 copy-start.5
  194.7 2.3 copy-start.11
  304.4 1.4 copy-start.7
  367.6 2.3 copy-start.2
  368.9 1.1 copy-start.3
  513.1 19.1 %copy-start.9 = (f32[8,128,128]{2,1,0:T(8,128)S(1)}, f32[8,128,128]{2,1,0:T(8,128)}, u32[]{:S(2)}) copy-start(f32[8,128,128]{2,1,0:T(8,128)} %param.10) | copy-start | bytes 1572868
  539.7 32.7 %all-to-all-start.5 = ((f32[1,2,128,8,128]{4,3,1,0,2:T(8,128)}), f32[1,2,128,8,128]{4,3,1,0,2:T(8,128)}, u32[]{:S(2)}, u32[]{:S(2)}) async-start(f32[1,2,128,8,128]{4,3,1,0,2:T(8,128)} %copy.135), calls=%async_computation.5 | async-start | bytes 2097152 | tf_op jit(solution)/shard_map/all_to_all | solution.py:106
  594.3 6.0 copy-start.10
  594.3 53.2 %all-to-all-start.6 = ((f32[2,2,8,128,128]{4,2,0,1,3:T(8,128)}), f32[2,2,8,128,128]{4,2,0,1,3:T(8,128)}, u32[]{:S(2)}, u32[]{:S(2)}) async-start(f32[2,2,8,128,128]{4,2,0,1,3:T(8,128)} %copy.145), calls=%async_computation.6 | async-start | bytes 4194304 | tf_op jit(solution)/shard_map/all_to_all | solution.py:103
  659.8 15.3 %copy-start.8 = (f32[8,128,128]{2,1,0:T(8,128)S(1)}, f32[8,128,128]{2,1,0:T(8,128)}, u32[]{:S(2)}) copy-start(f32[8,128,128]{2,1,0:T(8,128)} %param.9) | copy-start | bytes 1572868
Sparse Core Ops, SparseCore 0:
  514.3 17.9 all-reduce.6
